TPU v7x, 32 devices: a whole 2x2x4 slice. The times are simulated.
32 devices in a mesh: ctx: 16 (over z, x, core), fsdp: 2 (over y).
Axes of the slice: x: 2, y: 2, z: 4, core: 2. Of those that a mesh axis runs over, the one named last changes fastest.
Arguments:
- block_input: bfloat16 [2, 2048, 2048], P('fsdp', 'ctx'), may hold values from -36 to 36
- query_weight: bfloat16 [2048, 2048], P(('ctx', 'fsdp')), may hold values from -0.125 to 0.125
- key_weight: bfloat16 [2048, 1024], P(('ctx', 'fsdp')), may hold values from -0.125 to 0.125
- value_weight: bfloat16 [2048, 1024], P(('ctx', 'fsdp')), may hold values from -0.125 to 0.125
- output_weight: bfloat16 [2048, 2048], P(('ctx', 'fsdp')), may hold values from -0.375 to 0.375
- gate_weight: bfloat16 [2048, 6144], P(('ctx', 'fsdp')), may hold values from -0.125 to 0.125
- up_weight: bfloat16 [2048, 6144], P(('ctx', 'fsdp')), may hold values from -0.125 to 0.125
- down_weight: bfloat16 [2048, 6144], P(('ctx', 'fsdp')), may hold values from -0.078125 to 0.078125
- attn_gain: float32 [2048], replicated, may hold values from 0.5 to 1.5
- mlp_gain: float32 [2048], replicated, may hold values from 0.5 to 1.5
- query_gain: float32 [128], replicated, may hold values from 0.7 to 2.2
- key_gain: float32 [128], replicated, may hold values from 0.7 to 2.2
- block_order: int32 [32], replicated, may hold values from 0 to 31, each once
- cotangent: bfloat16 [2, 2048, 2048], P('fsdp', 'ctx'), may hold values from -18 to 18
Outputs:
- block_output: bfloat16 [2, 2048, 2048], P('fsdp', 'ctx')
- input_grad: float32 [2, 2048, 2048], P('fsdp', 'ctx')
- query_weight_grad: float32 [2048, 2048], P(('ctx', 'fsdp'))
- key_weight_grad: float32 [2048, 1024], P(('ctx', 'fsdp'))
- value_weight_grad: float32 [2048, 1024], P(('ctx', 'fsdp'))
- output_weight_grad: float32 [2048, 2048], P(('ctx', 'fsdp'))
- gate_weight_grad: float32 [2048, 6144], P(('ctx', 'fsdp'))
- up_weight_grad: float32 [2048, 6144], P(('ctx', 'fsdp'))
- down_weight_grad: float32 [2048, 6144], P(('ctx', 'fsdp'))
- attn_gain_grad: float32 [2048], replicated
- mlp_gain_grad: float32 [2048], replicated
- query_gain_grad: float32 [128], replicated
- key_gain_grad: float32 [128], replicated
Inputs may be any that keep to these rules, and one draw needn't show every extreme that they name: `block_order`: each value appears exactly once.
All inputs are finite; a program needn't handle non-finite values.
Results may differ from a plain program's by a relative error of at most 0.025.
Values may be sent and summed in bfloat16 or wider, within the bound.
No kernel may reach another device: no remote copies, remote signals or barrier semaphores. Data moves between devices by JAX's collectives and lax.ppermute only.
A program may use at most 512 MiB of HBM per device.

v0:
```python
import math
import jax
import jax.numpy as jnp
from jax import lax
from jax.sharding import PartitionSpec as P

eps_model = 1e-06
rope_base = 1000000.0


def inv_root(field):
    return lax.rsqrt(jnp.mean(field * field, axis=-1, keepdims=True) + eps_model)


def norm_back(field, factor, gain, grad_in):
    weighted = gain * grad_in
    inner_mean = jnp.mean(weighted * field, axis=-1, keepdims=True)
    return factor * weighted - field * (factor * factor * factor) * inner_mean


def rope_tables(positions, head_size):
    half_size = head_size // 2
    exponent = jnp.arange(half_size, dtype=jnp.float32) * jnp.float32(2.0 / head_size)
    inverse = jnp.exp(-exponent * jnp.float32(math.log(rope_base)))
    angles = positions.astype(jnp.float32)[:, None] * inverse[None, :]
    return (jnp.cos(angles)[:, None, :], jnp.sin(angles)[:, None, :])


def rotate(field, cosine, sine):
    first_half, second_half = jnp.split(field, 2, axis=-1)
    return jnp.concatenate(
        [first_half * cosine - second_half * sine, second_half * cosine + first_half * sine],
        axis=-1,
    )


def rotate_back(grad_in, cosine, sine):
    first_half, second_half = jnp.split(grad_in, 2, axis=-1)
    return jnp.concatenate(
        [first_half * cosine + second_half * sine, second_half * cosine - first_half * sine],
        axis=-1,
    )


def slot_positions(block_order, first_index, count, half_rows):
    row_index = first_index + jnp.arange(count, dtype=jnp.int32)
    slot_index = row_index // half_rows
    table = jnp.arange(block_order.shape[0], dtype=jnp.int32)
    picked = jnp.sum(
        jnp.where(slot_index[:, None] == table[None, :], block_order[None, :], 0), axis=1
    )
    return picked * half_rows + row_index % half_rows


def outer_rows(left, right):
    return lax.dot_general(
        left, right, (((0,), (0,)), ((), ())), preferred_element_type=jnp.float32
    )


def keep_state(state):
    return state


def stacked_terms(top_left, top_right, low_left, low_right):
    rows = top_left.shape[0]
    left = jnp.concatenate([top_left, low_left], axis=0)
    upper = jnp.concatenate(
        [top_right, jnp.zeros((rows, low_right.shape[1]), top_right.dtype)], axis=1
    )
    lower = jnp.concatenate(
        [jnp.zeros((rows, top_right.shape[1]), low_right.dtype), low_right], axis=1
    )
    return (left, jnp.concatenate([upper, lower], axis=0))


def shards(
    block_input,
    query_weight,
    key_weight,
    value_weight,
    output_weight,
    gate_weight,
    up_weight,
    down_weight,
    attn_gain,
    mlp_gain,
    query_gain,
    key_gain,
    block_order,
    cotangent,
):
    f32 = jnp.float32
    bf16 = jnp.bfloat16
    ctx_size = lax.axis_size("ctx")
    ctx_rank = lax.axis_index("ctx")
    tokens = block_input.shape[1]
    half_rows = tokens // 2
    head_size = query_gain.shape[0]
    heads = query_weight.shape[1] // head_size
    kv_heads = key_weight.shape[1] // head_size
    group = heads // kv_heads
    kv_width = kv_heads * head_size
    hidden_units = gate_weight.shape[1]
    score_scale = 1.0 / math.sqrt(head_size)
    step_cap = max(tokens, 1024)
    forward_weights = (
        lax.all_gather(query_weight, ("ctx", "fsdp"), axis=0, tiled=True),
        lax.all_gather(key_weight, ("ctx", "fsdp"), axis=0, tiled=True),
        lax.all_gather(value_weight, ("ctx", "fsdp"), axis=0, tiled=True),
        lax.all_gather(output_weight, ("ctx", "fsdp"), axis=0, tiled=True),
        lax.all_gather(gate_weight, ("ctx", "fsdp"), axis=0, tiled=True),
        lax.all_gather(up_weight, ("ctx", "fsdp"), axis=0, tiled=True),
        lax.all_gather(down_weight, ("ctx", "fsdp"), axis=0, tiled=True),
    )
    full_query, full_key, full_value, full_output, full_gate, full_up, full_down = forward_weights
    query_pos = slot_positions(block_order, ctx_rank * tokens, tokens, half_rows)
    cosine, sine = rope_tables(query_pos, head_size)
    inputs32 = block_input[0].astype(f32)
    scale_attn = inv_root(inputs32)
    normed_attn = (inputs32 * scale_attn * attn_gain).astype(bf16)
    query_raw = jnp.dot(normed_attn, full_query, preferred_element_type=f32).reshape(
        tokens, heads, head_size
    )
    key_raw = jnp.dot(normed_attn, full_key, preferred_element_type=f32).reshape(
        tokens, kv_heads, head_size
    )
    value_bf = jnp.dot(normed_attn, full_value, preferred_element_type=f32).astype(bf16)
    scale_query = inv_root(query_raw)
    scale_key = inv_root(key_raw)
    query_flat = (
        rotate(query_raw * scale_query * query_gain, cosine, sine)
        .astype(bf16)
        .reshape(tokens, kv_heads, group, head_size)
    )
    query_rot = jnp.transpose(query_flat, (1, 2, 0, 3))
    key_rot = rotate(key_raw * scale_key * key_gain, cosine, sine).astype(bf16)
    keyvals = jnp.concatenate([key_rot.reshape(tokens, kv_width), value_bf], axis=1)

    def attend_block(state, key_block, key_pos):
        weighted_sum, exp_total = state
        block_rows = key_block.shape[0]
        key_heads = key_block[:, :kv_width].reshape(block_rows, kv_heads, head_size)
        value_heads = key_block[:, kv_width:].reshape(block_rows, kv_heads, head_size)
        scores = (
            jnp.einsum("gjqd,kgd->gjqk", query_rot, key_heads, preferred_element_type=f32)
            * score_scale
        )
        allowed = key_pos[None, :] <= query_pos[:, None]
        exp_scores = jnp.where(allowed, jnp.exp(scores), 0.0)
        exp_total = exp_total + jnp.sum(exp_scores, axis=-1)
        weighted_sum = weighted_sum + jnp.einsum(
            "gjqk,kgd->gjqd", exp_scores.astype(bf16), value_heads, preferred_element_type=f32
        )
        return (weighted_sum, exp_total)

    start_sum = jnp.zeros((kv_heads, group, tokens, head_size), f32)
    start_total = jnp.zeros((kv_heads, group, tokens), f32)
    shard_rows = lax.all_gather(keyvals, "ctx", axis=0, tiled=True)
    row_count = shard_rows.shape[0]
    step_rows = math.gcd(row_count, step_cap)

    def turn_step(turn_index, state):
        first_row = turn_index * step_rows
        key_block = lax.dynamic_slice_in_dim(shard_rows, first_row, step_rows, 0)
        key_pos = slot_positions(block_order, first_row, step_rows, half_rows)
        return lax.cond(
            jnp.min(key_pos) <= jnp.max(query_pos),
            lambda inner: attend_block(inner, key_block, key_pos),
            keep_state,
            state,
        )

    weighted_sum, exp_total = lax.fori_loop(
        0, row_count // step_rows, turn_step, (start_sum, start_total)
    )
    attn_heads = weighted_sum / exp_total[..., None]
    attn_four = attn_heads.astype(bf16)
    attn_bf = jnp.transpose(attn_four, (2, 0, 1, 3)).reshape(tokens, heads * head_size)
    log_total = jnp.log(exp_total)
    hidden_one = inputs32 + jnp.einsum(
        "th,dh->td", attn_bf, full_output, preferred_element_type=f32
    )
    scale_mlp = inv_root(hidden_one)
    normed_mlp = (hidden_one * scale_mlp * mlp_gain).astype(bf16)
    gate_pre = jnp.dot(normed_mlp, full_gate, preferred_element_type=f32)
    up_pre = jnp.dot(normed_mlp, full_up, preferred_element_type=f32)
    activated = (jax.nn.silu(gate_pre) * up_pre).astype(bf16)
    block_out = (
        hidden_one + jnp.einsum("tf,df->td", activated, full_down, preferred_element_type=f32)
    ).astype(bf16)
    back_gate, back_up, back_down = (
        lax.all_gather(gate_weight, ("ctx", "fsdp"), axis=0, tiled=True),
        lax.all_gather(up_weight, ("ctx", "fsdp"), axis=0, tiled=True),
        lax.all_gather(down_weight, ("ctx", "fsdp"), axis=0, tiled=True),
    )
    grad_bf = cotangent[0]
    act_grad = jnp.dot(grad_bf, back_down, preferred_element_type=f32)
    sigma = jax.nn.sigmoid(gate_pre)
    gate_grad_in = (act_grad * up_pre * sigma * (1.0 + gate_pre * (1.0 - sigma))).astype(bf16)
    up_grad_in = (act_grad * gate_pre * sigma).astype(bf16)
    normed_mlp_grad = jnp.einsum(
        "tf,df->td", gate_grad_in, back_gate, preferred_element_type=f32
    ) + jnp.einsum("tf,df->td", up_grad_in, back_up, preferred_element_type=f32)
    mlp_gain_part = jnp.sum(normed_mlp_grad * hidden_one * scale_mlp, axis=0)
    hidden_grad = grad_bf.astype(f32) + norm_back(hidden_one, scale_mlp, mlp_gain, normed_mlp_grad)
    hidden_grad_bf = hidden_grad.astype(bf16)
    mlp_left, mlp_right = stacked_terms(
        normed_mlp, jnp.concatenate([gate_grad_in, up_grad_in], axis=1), grad_bf, activated
    )
    mlp_summed = lax.psum_scatter(
        outer_rows(mlp_left, mlp_right), ("ctx", "fsdp"), scatter_dimension=0, tiled=True
    )
    back_query, back_key, back_value, back_output = (
        lax.all_gather(query_weight, ("ctx", "fsdp"), axis=0, tiled=True),
        lax.all_gather(key_weight, ("ctx", "fsdp"), axis=0, tiled=True),
        lax.all_gather(value_weight, ("ctx", "fsdp"), axis=0, tiled=True),
        lax.all_gather(output_weight, ("ctx", "fsdp"), axis=0, tiled=True),
    )
    attn_grad = jnp.dot(hidden_grad_bf, back_output, preferred_element_type=f32).astype(bf16)
    grad_heads = jnp.transpose(attn_grad.reshape(tokens, kv_heads, group, head_size), (1, 2, 0, 3))
    delta_heads = jnp.sum(grad_heads.astype(f32) * attn_four.astype(f32), axis=-1)

    def block_grads(key_block, key_pos, query_grad):
        block_rows = key_block.shape[0]

        def work_block(grad_in):
            key_heads = key_block[:, :kv_width].reshape(block_rows, kv_heads, head_size)
            value_heads = key_block[:, kv_width:].reshape(block_rows, kv_heads, head_size)
            scores = (
                jnp.einsum("gjqd,kgd->gjqk", query_rot, key_heads, preferred_element_type=f32)
                * score_scale
            )
            allowed = key_pos[None, :] <= query_pos[:, None]
            probs = jnp.where(allowed, jnp.exp(scores - log_total[..., None]), 0.0)
            value_part = jnp.einsum(
                "gjqk,gjqd->kgd", probs.astype(bf16), grad_heads, preferred_element_type=f32
            )
            d_probs = jnp.einsum(
                "gjqd,kgd->gjqk", grad_heads, value_heads, preferred_element_type=f32
            )
            d_scores = (probs * (d_probs - delta_heads[..., None])).astype(bf16)
            grad_next = (
                grad_in
                + jnp.einsum("gjqk,kgd->gjqd", d_scores, key_heads, preferred_element_type=f32)
                * score_scale
            )
            key_part = (
                jnp.einsum("gjqk,gjqd->kgd", d_scores, query_rot, preferred_element_type=f32)
                * score_scale
            )
            return (
                grad_next,
                jnp.concatenate(
                    [
                        key_part.reshape(block_rows, kv_width),
                        value_part.reshape(block_rows, kv_width),
                    ],
                    axis=1,
                ),
            )

        def skip_block(grad_in):
            return (grad_in, jnp.zeros((block_rows, 2 * kv_width), f32))

        return lax.cond(jnp.min(key_pos) <= jnp.max(query_pos), work_block, skip_block, query_grad)

    zero_query = jnp.zeros((kv_heads, group, tokens, head_size), f32)
    start_buffer = jnp.zeros((tokens * ctx_size, 2 * kv_width), f32)
    fold_shard_rows = lax.all_gather(keyvals, "ctx", axis=0, tiled=True)
    row_count = fold_shard_rows.shape[0]
    fold_step_rows = math.gcd(row_count, step_cap)

    def turn_step(turn_index, state):
        query_grad, key_buffer = state
        first_row = turn_index * fold_step_rows
        key_block = lax.dynamic_slice_in_dim(fold_shard_rows, first_row, fold_step_rows, 0)
        key_pos = slot_positions(block_order, first_row, fold_step_rows, half_rows)
        query_grad, block_grad = block_grads(key_block, key_pos, query_grad)
        key_buffer = lax.dynamic_update_slice_in_dim(key_buffer, block_grad, first_row, 0)
        return (query_grad, key_buffer)

    query_grad, key_buffer = lax.fori_loop(
        0, row_count // fold_step_rows, turn_step, (zero_query, start_buffer)
    )
    key_grads = lax.psum_scatter(key_buffer, "ctx", scatter_dimension=0, tiled=True)
    query_flat_grad = jnp.transpose(query_grad, (2, 0, 1, 3)).reshape(tokens, heads, head_size)
    query_normed_grad = rotate_back(query_flat_grad, cosine, sine)
    key_normed_grad = rotate_back(
        key_grads[:, :kv_width].reshape(tokens, kv_heads, head_size), cosine, sine
    )
    query_gain_part = jnp.sum(query_normed_grad * query_raw * scale_query, axis=(0, 1))
    key_gain_part = jnp.sum(key_normed_grad * key_raw * scale_key, axis=(0, 1))
    query_pre_grad = (
        norm_back(query_raw, scale_query, query_gain, query_normed_grad)
        .reshape(tokens, heads * head_size)
        .astype(bf16)
    )
    key_pre_grad = (
        norm_back(key_raw, scale_key, key_gain, key_normed_grad)
        .reshape(tokens, kv_width)
        .astype(bf16)
    )
    value_pre_grad = key_grads[:, kv_width:].astype(bf16)
    normed_attn_grad = (
        jnp.einsum("th,dh->td", query_pre_grad, back_query, preferred_element_type=f32)
        + jnp.einsum("th,dh->td", key_pre_grad, back_key, preferred_element_type=f32)
        + jnp.einsum("th,dh->td", value_pre_grad, back_value, preferred_element_type=f32)
    )
    attn_gain_part = jnp.sum(normed_attn_grad * inputs32 * scale_attn, axis=0)
    input_grad = hidden_grad + norm_back(inputs32, scale_attn, attn_gain, normed_attn_grad)
    first_grads = jnp.concatenate([query_pre_grad, key_pre_grad, value_pre_grad], axis=1)
    attn_left, attn_right = stacked_terms(normed_attn, first_grads, hidden_grad_bf, attn_bf)
    attn_summed = lax.psum_scatter(
        outer_rows(attn_left, attn_right), ("ctx", "fsdp"), scatter_dimension=0, tiled=True
    )
    gain_sums = lax.psum(
        (attn_gain_part, mlp_gain_part, query_gain_part, key_gain_part), ("ctx", "fsdp")
    )
    query_cols = heads * head_size
    query_part = attn_summed[:, :query_cols]
    key_part = attn_summed[:, query_cols : query_cols + kv_width]
    value_part = attn_summed[:, query_cols + kv_width : query_cols + 2 * kv_width]
    output_part = attn_summed[:, query_cols + 2 * kv_width :]
    gate_part = mlp_summed[:, :hidden_units]
    up_part = mlp_summed[:, hidden_units : 2 * hidden_units]
    down_part = mlp_summed[:, 2 * hidden_units :]
    return (
        block_out[None],
        input_grad[None],
        query_part,
        key_part,
        value_part,
        output_part,
        gate_part,
        up_part,
        down_part,
        gain_sums[0],
        gain_sums[1],
        gain_sums[2],
        gain_sums[3],
    )


def solution(mesh):
    in_specs = (
        P("fsdp", "ctx", None),
        P(("ctx", "fsdp"), None),
        P(("ctx", "fsdp"), None),
        P(("ctx", "fsdp"), None),
        P(("ctx", "fsdp"), None),
        P(("ctx", "fsdp"), None),
        P(("ctx", "fsdp"), None),
        P(("ctx", "fsdp"), None),
        P(),
        P(),
        P(),
        P(),
        P(),
        P("fsdp", "ctx", None),
    )
    out_specs = (
        P("fsdp", "ctx", None),
        P("fsdp", "ctx", None),
        P(("ctx", "fsdp"), None),
        P(("ctx", "fsdp"), None),
        P(("ctx", "fsdp"), None),
        P(("ctx", "fsdp"), None),
        P(("ctx", "fsdp"), None),
        P(("ctx", "fsdp"), None),
        P(("ctx", "fsdp"), None),
        P(),
        P(),
        P(),
        P(),
    )
    return jax.shard_map(shards, mesh=mesh, in_specs=in_specs, out_specs=out_specs, check_vma=False)
```

profile of v0, /device:TPU:0, one launch (start us, length us, event | category | flops | bytes accessed | tf_op | source)
XLA Modules:
  0.0 2867.1 jit_solution(12603607756975838349)
XLA Ops:
  13.5 62.2 %all-gather.9.cloned.1.call-done = bf16[2048,1024]{1,0:T(8,128)(2,1)} async-done(((bf16[64,1024]{1,0:T(8,128)(2,1)}), bf16[2048,1024]{1,0:T(8,128)(2,1)}) %all-gather.9.cloned.1.call-update) | async-done | bytes 4194320 | tf_op jit(solution)/shard_map/all_gather | solution.py:109
  87.0 52.3 %all-gather.11.cloned.1.call-done = bf16[2048,1024]{1,0:T(8,128)(2,1)} async-done(((bf16[64,1024]{1,0:T(8,128)(2,1)}), bf16[2048,1024]{1,0:T(8,128)(2,1)}) %all-gather.11.cloned.1.call-update) | async-done | bytes 4194320 | tf_op jit(solution)/shard_map/all_gather | solution.py:110
  146.5 71.8 %all-gather.15.cloned.1.call-done = bf16[2048,2048]{1,0:T(8,128)(2,1)} async-done(((bf16[64,2048]{1,0:T(8,128)(2,1)}), bf16[2048,2048]{1,0:T(8,128)(2,1)}) %all-gather.15.cloned.1.call-update) | async-done | bytes 8388624 | tf_op jit(solution)/shard_map/all_gather | solution.py:108
  238.2 56.3 %all-gather.13.cloned.1.call-done = bf16[2048,2048]{1,0:T(8,128)(2,1)} async-done(((bf16[128,2048]{1,0:T(8,128)(2,1)}), bf16[2048,2048]{1,0:T(8,128)(2,1)}) %all-gather.13.cloned.1.call-update) | async-done | bytes 8388624 | tf_op jit(solution)/shard_map/all_gather | solution.py:159
  306.9 19.6 while.37
  327.0 46.1 %all-gather.17.cloned.1.call-done = bf16[2048,2048]{1,0:T(8,128)(2,1)} async-done(((bf16[64,2048]{1,0:T(8,128)(2,1)}), bf16[2048,2048]{1,0:T(8,128)(2,1)}) %all-gather.17.cloned.1.call-update) | async-done | bytes 8388624 | tf_op jit(solution)/shard_map/all_gather | solution.py:111
  379.7 149.4 %all-gather.21.cloned.1.call-done = bf16[2048,6144]{1,0:T(8,128)(2,1)} async-done(((bf16[64,6144]{1,0:T(8,128)(2,1)}), bf16[2048,6144]{1,0:T(8,128)(2,1)}) %all-gather.21.cloned.1.call-update) | async-done | bytes 25165840 | tf_op jit(solution)/shard_map/all_gather | solution.py:113
  529.2 13.2 fusion.114
  542.4 142.5 %all-gather.19.cloned.1.call-done = bf16[2048,6144]{1,0:T(8,128)(2,1)} async-done(((bf16[64,6144]{1,0:T(8,128)(2,1)}), bf16[2048,6144]{1,0:T(8,128)(2,1)}) %all-gather.19.cloned.1.call-update) | async-done | bytes 25165840 | tf_op jit(solution)/shard_map/all_gather | solution.py:112
  684.9 13.2 fusion.113
  698.1 142.5 %all-gather.23.cloned.1.call-done = bf16[2048,6144]{1,0:T(8,128)(2,1)} async-done(((bf16[64,6144]{1,0:T(8,128)(2,1)}), bf16[2048,6144]{1,0:T(8,128)(2,1)}) %all-gather.23.cloned.1.call-update) | async-done | bytes 25165840 | tf_op jit(solution)/shard_map/all_gather | solution.py:114
  840.7 14.9 multiply_convert_fusion
  855.6 14.6 fusion.115
  870.2 14.6 multiply_reduce_fusion.1
  900.3 53.7 %while.38 = (s32[]{:T(128)}, f32[8,2,128,128]{3,2,1,0:T(8,128)S(1)}, f32[2048,2048]{0,1:T(8,128)}, s32[32]{0:T(128)S(1)}, s32[]{:T(128)}, /*index=5*/s32[128]{0:...) while((s32[]{:T(128)}, ...), condition=%wide.region_20.21_spmd, body=%wide.region_15.20_spmd.sunk | while | flops 2709256192 | bytes 99009984 | solution.py:283
  902.5 16.4 conditional.5
  929.2 16.4 conditional.5
  957.6 173.2 %reduce-scatter.4.cloned.1.call-done = f32[128,2048]{0,1:T(8,128)} async-done(((f32[2048,2048]{0,1:T(8,128)}), f32[128,2048]{0,1:T(8,128)}) %reduce-scatter.4.cloned.1.call-update) | async-done | bytes 1048592 | tf_op jit(solution)/shard_map/reduce_scatter | solution.py:286
  1133.5 20.4 fusion.49
  1156.4 79.1 %fusion.37 = f32[2048,18432]{1,0:T(8,128)} fusion(bf16[128,6144]{1,0:T(8,128)(2,1)S(1)} %copy-done.9, bf16[128,6144]{1,0:T(8,128)(2,1)} %broadcast_in_dim.161, bf16[128,6144]{1,0:T(8,128)(2,1)} %get-tuple-element.687, bf16[128,6144]{1,0:T(8,128)(2,1)S(1)} %copy-done.8, bf16[128,2048]{1,0:T(8,128)(2,1)} %bitcast.183, bf16[128,2048]{1,0:T(8,128)(2,1)} %copy-done.10), kind=kOutput, calls=%fused_computation.63 | convolution fusion | flops 19376635904 | bytes 158334976 | tf_op jit(solution)/shard_map/dot_general | solution.py:56
  1244.0 14.1 fusion.61
  1264.4 43.7 %all-reduce.2 = (f32[2048]{0:T(1024)}, f32[2048]{0:T(1024)}, f32[128]{0:T(128)}, f32[128]{0:T(128)}) all-reduce(f32[2048]{0:T(1024)S(1)} %get-tuple-element.627, f32[2048]{0:T(1024)S(1)} %copy-done.38, f32[128]{0:T(128)S(1)} %get-tuple-element.623, f32[128]{0:T(128)S(1)} %get-tuple-element.629), channel_id=1, replica_groups=mesh['ctx'=16,'fsdp'=2] {'ctx','fsdp'}, use_global_device_ids=true, to_apply=%region_28.29 | all-reduce | flops 4352 | bytes 34816 | tf_op jit(solution)/shard_map/psum | solution.py:317
  1309.5 276.1 %reduce-scatter.6.cloned.1.call-done = f32[64,6144]{1,0:T(8,128)} async-done(((f32[2048,6144]{1,0:T(8,128)}), f32[64,6144]{1,0:T(8,128)}) %reduce-scatter.6.cloned.1.call-update) | async-done | bytes 1572880 | tf_op jit(solution)/shard_map/reduce_scatter | solution.py:314
  1589.7 1266.0 %reduce-scatter.8.cloned.1.call-done = f32[64,18432]{1,0:T(8,128)} async-done(((f32[2048,18432]{1,0:T(8,128)}), f32[64,18432]{1,0:T(8,128)}) %reduce-scatter.8.cloned.1.call-update) | async-done | bytes 4718608 | tf_op jit(solution)/shard_map/reduce_scatter | solution.py:211
  (220 shorter events, 195.2 us)
Async XLA Ops:
  7.2 68.5 %all-gather.9.cloned.1.call-start = ((), (), s32[]{:S(2)}) async-start(), calls=%async_computation.3 | async-start | bytes 4325376 | tf_op jit(solution)/shard_map/all_gather | solution.py:109
  7.9 131.3 %all-gather.11.cloned.1.call-start = ((), (), s32[]{:S(2)}) async-start(), calls=%async_computation.4 | async-start | bytes 4325376 | tf_op jit(solution)/shard_map/all_gather | solution.py:110
  8.7 209.7 %all-gather.15.cloned.1.call-start = ((), (), s32[]{:S(2)}) async-start(), calls=%async_computation.6 | async-start | bytes 8650752 | tf_op jit(solution)/shard_map/all_gather | solution.py:108
  9.4 285.1 %all-gather.13.cloned.1.call-start = ((), (), s32[]{:S(2)}) async-start(), calls=%async_computation.5 | async-start | bytes 8912896 | tf_op jit(solution)/shard_map/all_gather | solution.py:159
  12.0 218.7 %copy-start.40 = (f32[128]{0:T(128)}, f32[128]{0:T(128)S(1)}, u32[]{:S(2)}) copy-start(f32[128]{0:T(128)S(1)} %get-tuple-element.712) | copy-start | bytes 1540
  12.2 225.3 %copy-start.25 = (f32[128,64]{0,1:T(8,128)}, f32[128,64]{0,1:T(8,128)S(1)}, u32[]{:S(2)}) copy-start(f32[128,64]{0,1:T(8,128)S(1)} %get-tuple-element.709) | copy-start | bytes 98308
  12.2 225.3 %copy-start.27 = (f32[128,64]{0,1:T(8,128)}, f32[128,64]{0,1:T(8,128)S(1)}, u32[]{:S(2)}) copy-start(f32[128,64]{0,1:T(8,128)S(1)} %get-tuple-element.710) | copy-start | bytes 98308
  13.4 125.8 %copy-start.17 = (bf16[128,2048]{1,0:T(8,128)(2,1)}, bf16[128,2048]{1,0:T(8,128)(2,1)S(1)}, u32[]{:S(2)}) copy-start(bf16[128,2048]{1,0:T(8,128)(2,1)S(1)} %fusion.70) | copy-start | bytes 1572868
  143.0 230.1 %all-gather.17.cloned.1.call-start = ((), (), s32[]{:S(2)}) async-start(), calls=%async_computation.7 | async-start | bytes 8650752 | tf_op jit(solution)/shard_map/all_gather | solution.py:111
  143.6 385.6 %all-gather.21.cloned.1.call-start = ((), (), s32[]{:S(2)}) async-start(), calls=%async_computation.9 | async-start | bytes 25952256 | tf_op jit(solution)/shard_map/all_gather | solution.py:113
  144.2 540.7 %all-gather.19.cloned.1.call-start = ((), (), s32[]{:S(2)}) async-start(), calls=%async_computation.8 | async-start | bytes 25952256 | tf_op jit(solution)/shard_map/all_gather | solution.py:112
  144.9 695.7 %all-gather.23.cloned.1.call-start = ((), (), s32[]{:S(2)}) async-start(), calls=%async_computation.10 | async-start | bytes 25952256 | tf_op jit(solution)/shard_map/all_gather | solution.py:114
  145.7 985.1 %reduce-scatter.4.cloned.1.call-start = ((), (), s32[]{:S(2)}) async-start(), calls=%async_computation.11 | async-start | bytes 17825792 | tf_op jit(solution)/shard_map/reduce_scatter | solution.py:286
  379.5 505.4 %copy-start = (f32[128,2048]{1,0:T(8,128)}, f32[128,2048]{1,0:T(8,128)S(1)}, u32[]{:S(2)}) copy-start(f32[128,2048]{1,0:T(8,128)S(1)} %get-tuple-element.720) | copy-start | bytes 3145732
  379.7 305.2 %copy-start.10 = (bf16[128,2048]{1,0:T(8,128)(2,1)}, bf16[128,2048]{1,0:T(8,128)(2,1)S(1)}, u32[]{:S(2)}) copy-start(bf16[128,2048]{1,0:T(8,128)(2,1)S(1)} %multiply_convert_fusion.3) | copy-start | bytes 1572868
  954.0 631.6 %reduce-scatter.6.cloned.1.call-start = ((), (), s32[]{:S(2)}) async-start(), calls=%async_computation.12 | async-start | bytes 51904512 | tf_op jit(solution)/shard_map/reduce_scatter | solution.py:314
  955.4 176.6 %copy-start.14 = (f32[128,8,128]{0,2,1:T(8,128)S(1)}, f32[128,8,128]{0,2,1:T(8,128)}, u32[]{:S(2)}) copy-start(f32[128,8,128]{0,2,1:T(8,128)} %copy-done.13) | copy-start | bytes 1572868
  955.4 176.6 %copy-start.35 = (f32[128,8]{0,1:T(8,128)S(1)}, f32[128,8]{0,1:T(8,128)}, u32[]{:S(2)}) copy-start(f32[128,8]{0,1:T(8,128)} %copy-done.34) | copy-start | bytes 12292
  955.4 176.6 %copy-start.43 = (f32[128]{0:T(128)S(1)}, f32[128]{0:T(128)}, u32[]{:S(2)}) copy-start(f32[128]{0:T(128)} %param.33) | copy-start | bytes 1540
  956.8 175.4 %copy-start.39 = (f32[128,8]{0,1:T(8,128)S(1)}, f32[128,8]{0,1:T(8,128)}, u32[]{:S(2)}) copy-start(f32[128,8]{0,1:T(8,128)} %get-tuple-element.707) | copy-start | bytes 12292
  957.3 176.2 %copy-start.16 = (bf16[128,2048]{1,0:T(8,128)(2,1)S(1)}, bf16[128,2048]{1,0:T(8,128)(2,1)}, u32[]{:S(2)}) copy-start(bf16[128,2048]{1,0:T(8,128)(2,1)} %copy-done.15) | copy-start | bytes 1572868
  957.3 176.2 %copy-start.18 = (bf16[128,2048]{1,0:T(8,128)(2,1)S(1)}, bf16[128,2048]{1,0:T(8,128)(2,1)}, u32[]{:S(2)}) copy-start(bf16[128,2048]{1,0:T(8,128)(2,1)} %copy-done.17) | copy-start | bytes 1572868
  957.6 196.3 %copy-start.19 = (bf16[128,16,128]{0,2,1:T(8,128)(2,1)}, bf16[128,16,128]{0,2,1:T(8,128)(2,1)S(1)}, u32[]{:S(2)}) copy-start(bf16[128,16,128]{0,2,1:T(8,128)(2,1)S(1)} %subtract_convert_fusion) | copy-start | bytes 1572868
  1154.0 1701.7 %reduce-scatter.8.cloned.1.call-start = ((), (), s32[]{:S(2)}) async-start(), calls=%async_computation.13 | async-start | bytes 155713536 | tf_op jit(solution)/shard_map/reduce_scatter | solution.py:211
  (34 other events, 434.2 us)
Sparse Core Ops, SparseCore 0:
  10.9 64.7 all-gather.8
  78.6 60.6 all-gather.10
  142.4 75.9 all-gather.14
  220.9 73.4 all-gather.12
  297.4 75.6 all-gather.16
  375.9 153.2 all-gather.20
  532.1 152.8 all-gather.18
  687.8 152.8 all-gather.22
  954.1 176.7 reduce-scatter.3
  1154.1 431.4 reduce-scatter.5
  1592.0 1263.6 reduce-scatter.7
where the time goes:
time: 2870 us
  waiting for transfers between devices  2440 us (85%)
  matrix products  249 us (9%)
  local copies, waits for them, and re-layouts  84.8 us (3%)
  blocking collectives  43.7 us (2%)
    reduce_scatter x1, waiting for transfers between devices, shards(): lax.psum_scatter(outer_rows(mlp_left, mlp_right), ('ctx', 'fsdp'), scatte...  1270 us
    reduce_scatter x1, waiting for transfers between devices, shards(): lax.psum_scatter(outer_rows(attn_left, attn_right), ('ctx', 'fsdp'), scat...  276 us
    reduce_scatter x1, waiting for transfers between devices, shards(): lax.psum_scatter(key_buffer, 'ctx', scatter_dimension=0, tiled=True)  173 us
    all_gather x1, waiting for transfers between devices, shards(): lax.all_gather(up_weight, ('ctx', 'fsdp'), axis=0, tiled=True)  149 us
    all_gather x1, waiting for transfers between devices, shards(): lax.all_gather(down_weight, ('ctx', 'fsdp'), axis=0, tiled=True)  143 us
    all_gather x1, waiting for transfers between devices, shards(): lax.all_gather(gate_weight, ('ctx', 'fsdp'), axis=0, tiled=True)  143 us
    dot_general x2, matrix products, outer_rows(): lax.dot_general(left, right, (((0,), (0,)), ((), ())), preferred_element_...  99.6 us
    all_gather x1, waiting for transfers between devices, shards(): lax.all_gather(query_weight, ('ctx', 'fsdp'), axis=0, tiled=True)  71.8 us
  transfers between devices with their start and end apart: 11, of which 11 were waited for; matrix products, arithmetic and copies ran while one was open for 8% of the time, Pallas kernels for 0%

commit v1 on v0

--- a/solution.py
+++ b/solution.py
@@ -6,6 +6,30 @@
 
 eps_model = 1e-06
 rope_base = 1000000.0
+
+
+def obtain_the_trees(block_here, dimension_no):
+    block_here = jnp.moveaxis(block_here, 0, dimension_no)
+    y_new = block_here.shape
+    after = block_here.reshape(
+        *y_new[:dimension_no],
+        y_new[dimension_no] * y_new[dimension_no + 1],
+        *y_new[dimension_no + 2 :]
+    )
+    return after
+
+
+def seats_all_cover(shard_in, device_axis):
+    nd = lax.axis_size(device_axis)
+    f_now = shard_in[None]
+    for i in range(nd.bit_length() - 1):
+        outer = 1 << i
+        reply = lax.ppermute(f_now, device_axis, [(s, s ^ outer) for s in range(nd)])
+        last = jnp.stack([f_now, reply], axis=0)
+        arr_now = lax.axis_index(device_axis)
+        g_now = arr_now >> i & 1
+        f_now = jnp.where(g_now == 0, last, last[::-1]).reshape(-1, *shard_in.shape)
+    return f_now
 
 
 def inv_root(field):
@@ -90,6 +114,12 @@
     block_order,
     cotangent,
 ):
+
+    def hold_tails(where_dim, block_in, arr_in):
+        near = seats_all_cover(arr_in, block_in)
+        part_now = obtain_the_trees(near, where_dim)
+        return part_now
+
     f32 = jnp.float32
     bf16 = jnp.bfloat16
     ctx_size = lax.axis_size("ctx")
@@ -110,7 +140,7 @@
         lax.all_gather(value_weight, ("ctx", "fsdp"), axis=0, tiled=True),
         lax.all_gather(output_weight, ("ctx", "fsdp"), axis=0, tiled=True),
         lax.all_gather(gate_weight, ("ctx", "fsdp"), axis=0, tiled=True),
-        lax.all_gather(up_weight, ("ctx", "fsdp"), axis=0, tiled=True),
+        hold_tails(0, ("ctx", "fsdp"), up_weight),
         lax.all_gather(down_weight, ("ctx", "fsdp"), axis=0, tiled=True),
     )
     full_query, full_key, full_value, full_output, full_gate, full_up, full_down = forward_weights

time: 2870 us -> 3450 us (1.20)
  waiting for transfers between devices: 2440 us -> 2960 us
  other arithmetic: 25.1 us -> 80.2 us
    ppermute x0 -> x5, waiting for transfers between devices: none -> 929 us  [seats_all_cover(): lax.ppermute(f_now, device_axis, [(s, s ^ outer) for s in range(nd)])]
    all_gather x1, waiting for transfers between devices: 143 us -> 0.01 us  [shards(): lax.all_gather(down_weight, ('ctx', 'fsdp'), axis=0, tiled=True)]
    all_gather x1, waiting for transfers between devices: 71.8 us -> 0.01 us  [shards(): lax.all_gather(query_weight, ('ctx', 'fsdp'), axis=0, tiled=True)]
    all_gather x1, waiting for transfers between devices: 143 us -> 83.1 us  [shards(): lax.all_gather(gate_weight, ('ctx', 'fsdp'), axis=0, tiled=True)]
    all_gather x1, waiting for transfers between devices: 56.3 us -> 0.02 us  [shards(): shard_rows = lax.all_gather(keyvals, 'ctx', axis=0, tiled=True)]
    all_gather x1, waiting for transfers between devices: 46.1 us -> 0.02 us  [shards(): lax.all_gather(output_weight, ('ctx', 'fsdp'), axis=0, tiled=True)]
  transfers between devices with their start and end apart: 11 -> 16, of which waited for: 11 -> 12; matrix products, arithmetic and copies ran while one was open for 8% -> 9% of each run, Pallas kernels for 0% -> 0%
where the time goes in v1:
time: 3450 us; the launch traced here: 3440 us
  waiting for transfers between devices  2960 us (86%)
  matrix products  244 us (7%)
  local copies, waits for them, and re-layouts  85.5 us (2%)
  other arithmetic  80.2 us (2%)
  blocking collectives  43.7 us (1%)
    reduce_scatter x1, waiting for transfers between devices, shards(): lax.psum_scatter(outer_rows(mlp_left, mlp_right), ('ctx', 'fsdp'), scatte...  1270 us
    ppermute x5, waiting for transfers between devices, seats_all_cover(): lax.ppermute(f_now, device_axis, [(s, s ^ outer) for s in range(nd)])  929 us
    reduce_scatter x1, waiting for transfers between devices, shards(): lax.psum_scatter(outer_rows(attn_left, attn_right), ('ctx', 'fsdp'), scat...  276 us
    reduce_scatter x1, waiting for transfers between devices, shards(): lax.psum_scatter(key_buffer, 'ctx', scatter_dimension=0, tiled=True)  173 us
    all_gather x1, waiting for transfers between devices, shards(): lax.all_gather(up_weight, ('ctx', 'fsdp'), axis=0, tiled=True)  118 us
    dot_general x2, matrix products, outer_rows(): lax.dot_general(left, right, (((0,), (0,)), ((), ())), preferred_element_...  99.6 us
    all_gather x1, waiting for transfers between devices, shards(): lax.all_gather(gate_weight, ('ctx', 'fsdp'), axis=0, tiled=True)  83.1 us
  transfers between devices with their start and end apart: 16, of which 12 were waited for; matrix products, arithmetic and copies ran while one was open for 9% of the time, Pallas kernels for 0%

profile of v1, /device:TPU:0, one launch (start us, length us, event | category | flops | bytes accessed | tf_op | source)
XLA Modules:
  0.0 3443.0 jit_solution(17803438293891015714)
XLA Ops:
  13.6 62.1 %all-gather.9.cloned.1.call-done = bf16[2048,1024]{1,0:T(8,128)(2,1)} async-done(((bf16[64,1024]{1,0:T(8,128)(2,1)}), bf16[2048,1024]{1,0:T(8,128)(2,1)}) %all-gather.9.cloned.1.call-update) | async-done | bytes 4194320 | tf_op jit(solution)/shard_map/all_gather | solution.py:139
  87.3 52.0 %all-gather.11.cloned.1.call-done = bf16[2048,1024]{1,0:T(8,128)(2,1)} async-done(((bf16[64,1024]{1,0:T(8,128)(2,1)}), bf16[2048,1024]{1,0:T(8,128)(2,1)}) %all-gather.11.cloned.1.call-update) | async-done | bytes 4194320 | tf_op jit(solution)/shard_map/all_gather | solution.py:140
  147.3 20.1 collective-permute-done
  178.1 89.8 %collective-permute-done.2 = bf16[4,64,6144]{2,1,0:T(8,128)(2,1)} collective-permute-done((bf16[4,64,6144]{2,1,0:T(8,128)(2,1)}, bf16[4,64,6144]{2,1,0:T(8,128)(2,1)}, u32[]{:S(2)}, u32[]{:S(2)}) %collective-permute-start.2) | collective-permute-done | bytes 3145760 | tf_op jit(solution)/shard_map/ppermute | solution.py:27
  277.3 223.0 %collective-permute-done.3 = bf16[8,64,6144]{2,1,0:T(8,128)(2,1)} collective-permute-done((bf16[8,64,6144]{2,1,0:T(8,128)(2,1)}, bf16[8,64,6144]{2,1,0:T(8,128)(2,1)}, u32[]{:S(2)}, u32[]{:S(2)}) %collective-permute-start.3) | collective-permute-done | bytes 6291488 | tf_op jit(solution)/shard_map/ppermute | solution.py:27
  547.6 19.5 while.37
  575.1 592.0 %collective-permute-done.4 = bf16[16,64,6144]{2,1,0:T(8,128)(2,1)} collective-permute-done((bf16[16,64,6144]{2,1,0:T(8,128)(2,1)}, bf16[16,64,6144]{2,1,0:T(8,128)(2,1)}, u32[]{:S(2)}, u32[]{:S(2)}) %collective-permute-start.4) | collective-permute-done | bytes 12582944 | tf_op jit(solution)/shard_map/ppermute | solution.py:27
  1179.5 13.9 reverse_select_fusion
  1193.4 13.4 fusion.98
  1206.8 83.1 %all-gather.19.cloned.1.call-done = bf16[2048,6144]{1,0:T(8,128)(2,1)} async-done(((bf16[64,6144]{1,0:T(8,128)(2,1)}), bf16[2048,6144]{1,0:T(8,128)(2,1)}) %all-gather.19.cloned.1.call-update) | async-done | bytes 25165840 | tf_op jit(solution)/shard_map/all_gather | solution.py:142
  1300.1 12.5 multiply_convert_fusion
  1312.6 14.7 fusion.116
  1327.3 118.5 %all-gather.23.cloned.1.call-done = bf16[2048,6144]{1,0:T(8,128)(2,1)} async-done(((bf16[64,6144]{1,0:T(8,128)(2,1)}), bf16[2048,6144]{1,0:T(8,128)(2,1)}) %all-gather.23.cloned.1.call-update) | async-done | bytes 25165840 | tf_op jit(solution)/shard_map/all_gather | solution.py:224
  1445.8 14.6 multiply_reduce_fusion.1
  1475.7 53.7 %while.38 = (s32[]{:T(128)}, f32[8,2,128,128]{3,2,1,0:T(8,128)S(1)}, f32[2048,2048]{0,1:T(8,128)}, s32[32]{0:T(128)S(1)}, s32[]{:T(128)}, /*index=5*/s32[128]{0:...) while((s32[]{:T(128)}, ...), condition=%wide.region_20.21_spmd, body=%wide.region_15.20_spmd.sunk | while | flops 2709256192 | bytes 99009984 | solution.py:313
  1478.0 16.4 conditional.5
  1504.7 16.4 conditional.5
  1532.9 173.5 %reduce-scatter.4.cloned.1.call-done = f32[128,2048]{0,1:T(8,128)} async-done(((f32[2048,2048]{0,1:T(8,128)}), f32[128,2048]{0,1:T(8,128)}) %reduce-scatter.4.cloned.1.call-update) | async-done | bytes 1048592 | tf_op jit(solution)/shard_map/reduce_scatter | solution.py:316
  1709.7 20.5 fusion.49
  1732.6 79.1 %fusion.37 = f32[2048,18432]{1,0:T(8,128)} fusion(bf16[128,6144]{1,0:T(8,128)(2,1)S(1)} %copy-done.11, bf16[128,6144]{1,0:T(8,128)(2,1)} %broadcast_in_dim.165, bf16[128,6144]{1,0:T(8,128)(2,1)} %get-tuple-element.687, bf16[128,6144]{1,0:T(8,128)(2,1)S(1)} %copy-done.10, bf16[128,2048]{1,0:T(8,128)(2,1)} %bitcast.193, bf16[128,2048]{1,0:T(8,128)(2,1)} %copy-done.19), kind=kOutput, calls=%fused_computation.68 | convolution fusion | flops 19376635904 | bytes 158334976 | tf_op jit(solution)/shard_map/dot_general | solution.py:80
  1820.2 14.1 fusion.61
  1840.6 43.7 %all-reduce.2 = (f32[2048]{0:T(1024)}, f32[2048]{0:T(1024)}, f32[128]{0:T(128)}, f32[128]{0:T(128)}) all-reduce(f32[2048]{0:T(1024)S(1)} %get-tuple-element.627, f32[2048]{0:T(1024)S(1)} %copy-done.41, f32[128]{0:T(128)S(1)} %get-tuple-element.623, f32[128]{0:T(128)S(1)} %get-tuple-element.629), channel_id=1, replica_groups=mesh['ctx'=16,'fsdp'=2] {'ctx','fsdp'}, use_global_device_ids=true, to_apply=%region_28.29 | all-reduce | flops 4352 | bytes 34816 | tf_op jit(solution)/shard_map/psum | solution.py:347
  1885.6 276.1 %reduce-scatter.6.cloned.1.call-done = f32[64,6144]{1,0:T(8,128)} async-done(((f32[2048,6144]{1,0:T(8,128)}), f32[64,6144]{1,0:T(8,128)}) %reduce-scatter.6.cloned.1.call-update) | async-done | bytes 1572880 | tf_op jit(solution)/shard_map/reduce_scatter | solution.py:344
  2165.8 1265.6 %reduce-scatter.8.cloned.1.call-done = f32[64,18432]{1,0:T(8,128)} async-done(((f32[2048,18432]{1,0:T(8,128)}), f32[64,18432]{1,0:T(8,128)}) %reduce-scatter.8.cloned.1.call-update) | async-done | bytes 4718608 | tf_op jit(solution)/shard_map/reduce_scatter | solution.py:241
  (244 shorter events, 255.4 us)
Async XLA Ops:
  7.2 68.5 %all-gather.9.cloned.1.call-start = ((), (), s32[]{:S(2)}) async-start(), calls=%async_computation.3 | async-start | bytes 4325376 | tf_op jit(solution)/shard_map/all_gather | solution.py:139
  7.9 131.3 %all-gather.11.cloned.1.call-start = ((), (), s32[]{:S(2)}) async-start(), calls=%async_computation.4 | async-start | bytes 4325376 | tf_op jit(solution)/shard_map/all_gather | solution.py:140
  8.7 506.7 %all-gather.15.cloned.1.call-start = ((), (), s32[]{:S(2)}) async-start(), calls=%async_computation.6 | async-start | bytes 8650752 | tf_op jit(solution)/shard_map/all_gather | solution.py:138
  9.4 525.7 %all-gather.13.cloned.1.call-start = ((), (), s32[]{:S(2)}) async-start(), calls=%async_computation.5 | async-start | bytes 8912896 | tf_op jit(solution)/shard_map/all_gather | solution.py:189
  12.1 515.6 %copy-start.43 = (f32[128]{0:T(128)}, f32[128]{0:T(128)S(1)}, u32[]{:S(2)}) copy-start(f32[128]{0:T(128)S(1)} %get-tuple-element.714) | copy-start | bytes 1540
  12.3 522.3 %copy-start.29 = (f32[128,64]{0,1:T(8,128)}, f32[128,64]{0,1:T(8,128)S(1)}, u32[]{:S(2)}) copy-start(f32[128,64]{0,1:T(8,128)S(1)} %get-tuple-element.711) | copy-start | bytes 98308
  12.3 522.2 %copy-start.31 = (f32[128,64]{0,1:T(8,128)}, f32[128,64]{0,1:T(8,128)S(1)}, u32[]{:S(2)}) copy-start(f32[128,64]{0,1:T(8,128)S(1)} %get-tuple-element.712) | copy-start | bytes 98308
  143.0 424.6 %all-gather.17.cloned.1.call-start = ((), (), s32[]{:S(2)}) async-start(), calls=%async_computation.7 | async-start | bytes 8650752 | tf_op jit(solution)/shard_map/all_gather | solution.py:141
  143.6 1049.8 %all-gather.21.cloned.1.call-start = ((), (), s32[]{:S(2)}) async-start(), calls=%async_computation.9 | async-start | bytes 25952256 | tf_op jit(solution)/shard_map/all_gather | solution.py:144
  144.2 1145.8 %all-gather.19.cloned.1.call-start = ((), (), s32[]{:S(2)}) async-start(), calls=%async_computation.8 | async-start | bytes 25952256 | tf_op jit(solution)/shard_map/all_gather | solution.py:142
  144.9 1300.8 %all-gather.23.cloned.1.call-start = ((), (), s32[]{:S(2)}) async-start(), calls=%async_computation.10 | async-start | bytes 25952256 | tf_op jit(solution)/shard_map/all_gather | solution.py:224
  145.7 1560.7 %reduce-scatter.4.cloned.1.call-start = ((), (), s32[]{:S(2)}) async-start(), calls=%async_computation.11 | async-start | bytes 17825792 | tf_op jit(solution)/shard_map/reduce_scatter | solution.py:316
  145.7 21.6 collective-permute-start
  169.1 3.8 collective-permute-start.1
  176.9 91.0 %collective-permute-start.2 = (bf16[4,64,6144]{2,1,0:T(8,128)(2,1)}, bf16[4,64,6144]{2,1,0:T(8,128)(2,1)}, u32[]{:S(2)}, u32[]{:S(2)}) collective-permute-start(bf16[4,64,6144]{2,1,0:T(8,128)(2,1)} %bitcast.40), channel_id=1, source_target_pairs={{0,4},{1,5},{2,6},{3,7},{4,0},{5,1},{6,2},{7,3},{8,12},{9,13},{10,... | collective-permute-start | bytes 9437192 | tf_op jit(solution)/shard_map/ppermute | solution.py:27
  275.6 224.7 %collective-permute-start.3 = (bf16[8,64,6144]{2,1,0:T(8,128)(2,1)}, bf16[8,64,6144]{2,1,0:T(8,128)(2,1)}, u32[]{:S(2)}, u32[]{:S(2)}) collective-permute-start(bf16[8,64,6144]{2,1,0:T(8,128)(2,1)} %bitcast.43), channel_id=1, source_target_pairs={{0,8},{1,9},{2,10},{3,11},{4,12},{5,13},{6,14},{7,15},{8,0},{9,1},... | collective-permute-start | bytes 18874376 | tf_op jit(solution)/shard_map/ppermute | solution.py:27
  514.6 652.4 %collective-permute-start.4 = (bf16[16,64,6144]{2,1,0:T(8,128)(2,1)}, bf16[16,64,6144]{2,1,0:T(8,128)(2,1)}, u32[]{:S(2)}, u32[]{:S(2)}) collective-permute-start(bf16[16,64,6144]{2,1,0:T(8,128)(2,1)} %bitcast.46), channel_id=1, source_target_pairs={{0,16},{1,17},{2,18},{3,19},{4,20},{5,21},{6,22},{7,23},{8,24},{9,... | collective-permute-start | bytes 37748744 | tf_op jit(solution)/shard_map/ppermute | solution.py:27
  574.8 885.5 %copy-start.2 = (f32[128,2048]{1,0:T(8,128)}, f32[128,2048]{1,0:T(8,128)S(1)}, u32[]{:S(2)}) copy-start(f32[128,2048]{1,0:T(8,128)S(1)} %get-tuple-element.722) | copy-start | bytes 3145732
  575.0 714.9 %copy-start.19 = (bf16[128,2048]{1,0:T(8,128)(2,1)}, bf16[128,2048]{1,0:T(8,128)(2,1)S(1)}, u32[]{:S(2)}) copy-start(bf16[128,2048]{1,0:T(8,128)(2,1)S(1)} %multiply_convert_fusion.3) | copy-start | bytes 1572868
  1529.5 632.2 %reduce-scatter.6.cloned.1.call-start = ((), (), s32[]{:S(2)}) async-start(), calls=%async_computation.12 | async-start | bytes 51904512 | tf_op jit(solution)/shard_map/reduce_scatter | solution.py:344
  1530.7 179.0 %copy-start.17 = (bf16[128,2048]{1,0:T(8,128)(2,1)S(1)}, bf16[128,2048]{1,0:T(8,128)(2,1)}, u32[]{:S(2)}) copy-start(bf16[128,2048]{1,0:T(8,128)(2,1)} %copy-done.16) | copy-start | bytes 1572868
  1530.7 179.0 %copy-start.21 = (bf16[128,2048]{1,0:T(8,128)(2,1)S(1)}, bf16[128,2048]{1,0:T(8,128)(2,1)}, u32[]{:S(2)}) copy-start(bf16[128,2048]{1,0:T(8,128)(2,1)} %copy-done.20) | copy-start | bytes 1572868
  1532.9 197.3 %copy-start.22 = (bf16[128,16,128]{0,2,1:T(8,128)(2,1)}, bf16[128,16,128]{0,2,1:T(8,128)(2,1)S(1)}, u32[]{:S(2)}) copy-start(bf16[128,16,128]{0,2,1:T(8,128)(2,1)S(1)} %subtract_convert_fusion) | copy-start | bytes 1572868
  1730.2 1701.2 %reduce-scatter.8.cloned.1.call-start = ((), (), s32[]{:S(2)}) async-start(), calls=%async_computation.13 | async-start | bytes 155713536 | tf_op jit(solution)/shard_map/reduce_scatter | solution.py:241
  (41 other events, 1273.2 us)
Sparse Core Ops, SparseCore 0:
  10.9 64.7 all-gather.8
  78.6 60.6 all-gather.10
  142.4 92.9 all-gather.14
  237.9 98.5 all-gather.12
  339.4 112.3 all-gather.16
  454.6 483.3 all-gather.20
  940.9 349.0 all-gather.18
  1292.8 152.8 all-gather.22
  1529.6 176.7 reduce-scatter.3
  1730.3 431.3 reduce-scatter.5
  2168.1 1263.2 reduce-scatter.7
